TPU v7x, 256 devices: a whole 4x4x8 slice. The times are simulated.
256 devices in a mesh: blk: 16 (over x, y_lo, core), lane: 16 (over y_hi, z).
Axes of the slice: x: 4, y: 4 (y_hi: 2, y_lo: 2; y = y_hi * 2 + y_lo), z: 8, core: 2. Of those that a mesh axis runs over, the one named last changes fastest.
Arguments:
- recv_pos: float32 [3, 32768], P(None, ('blk', 'lane')), may hold values from 0 to 6
- recv_angles: float32 [2, 32768], P(None, ('blk', 'lane')), may hold values from -3.140625 to 3.140625
- src_pos: float32 [3, 262144], P(None, ('blk', 'lane')), may hold values from 0 to 6
- src_angles: float32 [2, 262144], P(None, ('blk', 'lane')), may hold values from -3.140625 to 3.140625
- src_area: float32 [262144], P(('blk', 'lane')), may hold values from 0.02 to 0.08
- reemission: float32 [262144], P(('blk', 'lane')), may hold values from 0.1 to 0.9
- incident: bfloat16 [262144, 128], P(('blk', 'lane')), may hold values from 0 to 2
- direct: float32 [32768, 128], P(('blk', 'lane')), may hold values from 0.5 to 1.5
- visible_lists: int32 [16, 16, 16, 16, 4], P('blk', 'lane'), may hold values from 0 to 7, as said below
- visible_counts: int32 [16, 16, 16, 16], P('blk', 'lane'), may hold values from 0 to 4, as said below
Outputs:
- incoming: float32 [32768, 128], P(('blk', 'lane'))
Inputs may be any that keep to these rules, and one draw needn't show every extreme that they name: `visible_lists`: each list names 4 different local source blocks of its device; entries at slots at or past the count are valid but unused. `visible_counts`: some list holds exactly 4 used entries in every draw; the loads differ from device to device.
All inputs are finite; a program needn't handle non-finite values.
Results may differ from a plain program's by a relative error of at most 0.0003.
Values sent between devices are 32-bit elements; how exact they have to be, the bound alone decides.
No kernel may reach another device: no remote copies, remote signals or barrier semaphores. Data moves between devices by JAX's collectives and lax.ppermute only.
A program may use at most 64 MiB of HBM per device.

v0:
```python
import jax
import jax.numpy as jnp
from jax import lax
from jax.sharding import PartitionSpec as P


def shifted(block, axis, distance):
    devices = range(lax.axis_size(axis))
    route = [((i - distance) % len(devices), i) for i in devices]
    return lax.ppermute(block, axis, route)


def normals(angle_rows):
    polar = angle_rows[0]
    azimuth = angle_rows[1]
    return jnp.stack(
        [jnp.sin(polar) * jnp.cos(azimuth), jnp.sin(polar) * jnp.sin(azimuth), jnp.cos(polar)]
    )


def factors(receiver_pos, receiver_dir, source_pos, source_dir, source_area, source_keep):
    offsets = [source_pos[component] - receiver_pos[component] for component in range(3)]
    distance = offsets[0] * offsets[0] + offsets[1] * offsets[1] + offsets[2] * offsets[2]
    facing = jnp.maximum(
        receiver_dir[0] * offsets[0] + receiver_dir[1] * offsets[1] + receiver_dir[2] * offsets[2],
        0.0,
    )
    seen = jnp.maximum(
        -(source_dir[0] * offsets[0] + source_dir[1] * offsets[1] + source_dir[2] * offsets[2]), 0.0
    )
    spread = distance + source_area
    value = source_keep * source_area * facing * seen / (jnp.pi * spread * spread)
    return value.astype(jnp.bfloat16)


def shards(
    recv_pos,
    recv_angles,
    src_pos,
    src_angles,
    src_area,
    reemission,
    incident,
    direct,
    visible_lists,
    visible_counts,
):
    group_count = lax.axis_size("blk")
    lane_count = lax.axis_size("lane")
    block_rows = recv_pos.shape[1]
    bin_count = incident.shape[1]
    source_blocks = src_area.shape[0] // block_rows
    slot_count = visible_lists.shape[-1]
    every_pos, every_angles = (
        lax.all_gather(recv_pos, ("blk", "lane"), axis=1, tiled=True),
        lax.all_gather(recv_angles, ("blk", "lane"), axis=1, tiled=True),
    )
    receiver_pos = every_pos.reshape(3, group_count * lane_count, block_rows)
    receiver_dir = normals(every_angles).reshape(3, group_count * lane_count, block_rows)
    source_pos = src_pos.reshape(3, source_blocks, block_rows)
    source_dir = normals(src_angles).reshape(3, source_blocks, block_rows)
    source_area = src_area.reshape(source_blocks, block_rows)
    source_keep = reemission.reshape(source_blocks, block_rows)
    emission = incident.reshape(source_blocks, block_rows, bin_count)
    my_lists = visible_lists[0, 0]
    my_counts = visible_counts[0, 0]
    group_index = lax.axis_index("blk")
    lane_range = jnp.arange(lane_count, dtype=jnp.int32)
    slot_range = jnp.arange(slot_count, dtype=jnp.int32)

    def slab_of(cycle_step):
        ahead = (group_index - cycle_step - 1) % group_count
        return ahead + 0 * lane_range

    def contribution(cycle_step):
        slabs = slab_of(cycle_step)
        targets = slabs * lane_count + lane_range
        near_pos = jnp.take(receiver_pos, targets, axis=1)
        near_dir = jnp.take(receiver_dir, targets, axis=1)
        chosen = my_lists[slabs, lane_range]
        counts_here = my_counts[slabs, lane_range]
        picked_pos = source_pos[:, chosen]
        picked_dir = source_dir[:, chosen]
        picked_area = source_area[chosen]
        picked_keep = source_keep[chosen]
        picked_flux = emission[chosen]
        values = factors(
            near_pos[:, :, :, None, None],
            near_dir[:, :, :, None, None],
            picked_pos[:, :, None, :, :],
            picked_dir[:, :, None, :, :],
            picked_area[:, None, :, :],
            picked_keep[:, None, :, :],
        )
        live_mask = (slot_range[None, :] < counts_here[:, None])[:, None, :, None]
        values = jnp.where(live_mask, values, jnp.zeros((), jnp.bfloat16))
        return jnp.einsum("jrcs,jcsb->jrb", values, picked_flux, preferred_element_type=jnp.float32)

    def pass_on(running):
        return shifted(running, "blk", 1)

    def cycle_turn(cycle_step, running):
        return pass_on(running + contribution(cycle_step))

    start = jnp.zeros((lane_count, block_rows, bin_count), jnp.float32)
    running = lax.fori_loop(0, group_count - 1, cycle_turn, start)
    running = running + contribution(group_count - 1)
    owned = lax.psum_scatter(
        running.reshape(lane_count * block_rows, bin_count), "lane", scatter_dimension=0, tiled=True
    )
    return direct + owned


def solution(mesh):
    return jax.shard_map(
        shards,
        mesh=mesh,
        in_specs=(
            P(None, ("blk", "lane")),
            P(None, ("blk", "lane")),
            P(None, ("blk", "lane")),
            P(None, ("blk", "lane")),
            P(("blk", "lane")),
            P(("blk", "lane")),
            P(("blk", "lane"), None),
            P(("blk", "lane"), None),
            P("blk", "lane", None, None, None),
            P("blk", "lane", None, None),
        ),
        out_specs=P(("blk", "lane"), None),
        check_vma=False,
    )
```

profile of v0, /device:TPU:2, one launch (start us, length us, event | category | flops | bytes accessed | tf_op | source)
XLA Modules:
  0.0 2028.8 jit_solution(4897555335530008646)
XLA Ops:
  7.5 562.1 %all_gather.6 = f32[2,32768]{1,0:T(2,128)S(1)} all-gather(f32[2,128]{1,0:T(2,128)} %param.15), channel_id=1, replica_groups=mesh['blk'=16,'lane'=16] {'blk','lane'}, dimensions={1}, use_global_device_ids=true | all-gather | bytes 263168 | tf_op jit(solution)/shard_map/all_gather | solution.py:56
  577.1 593.8 %all_gather.7 = f32[3,32768]{1,0:T(4,128)} all-gather(f32[3,128]{1,0:T(4,128)} %param.14), channel_id=1, replica_groups=mesh['blk'=16,'lane'=16] {'blk','lane'}, dimensions={1}, use_global_device_ids=true | all-gather | bytes 394752 | tf_op jit(solution)/shard_map/all_gather | solution.py:55
  1184.7 602.5 %while.17 = (s32[]{:T(128)}, f32[16,128,128]{2,1,0:T(8,128)}, s32[]{:T(128)}, s32[16,16]{1,0:T(8,128)S(1)}, s32[16,16,4]{2,1,0:T(8,128)S(1)}, /*index=5*/f32[8,1...) while((s32[]{:T(128)}, f32[16,128,128]{2,1,0:T(8,128)}, ...), condition=%wide.region_1.3_spmd.clone.clone, body=%wide.region_0.2_spmd.clone.clone.sunk | while | flops 299129344 | bytes 18412892 | solution.py:106
  1192.4 8.1 fusion.118
  1200.7 39.9 %collective-permute-done = f32[16,128,128]{2,1,0:T(8,128)S(1)} collective-permute-done((f32[16,128,128]{2,1,0:T(8,128)}, f32[16,128,128]{2,1,0:T(8,128)S(1)}, u32[]{:S(2)}, u32[]{:S(2)}) %collective-permute-start) | collective-permute-done | bytes 1048608 | tf_op jit(solution)/shard_map/while/body/eval_jaxpr/ppermute | solution.py:10
  1249.2 8.1 fusion.118
  1257.3 34.7 %collective-permute-done = f32[16,128,128]{2,1,0:T(8,128)S(1)} collective-permute-done((f32[16,128,128]{2,1,0:T(8,128)}, f32[16,128,128]{2,1,0:T(8,128)S(1)}, u32[]{:S(2)}, u32[]{:S(2)}) %collective-permute-start) | collective-permute-done | bytes 1048608 | tf_op jit(solution)/shard_map/while/body/eval_jaxpr/ppermute | solution.py:10
  1300.7 8.1 fusion.118
  1308.8 59.2 %collective-permute-done = f32[16,128,128]{2,1,0:T(8,128)S(1)} collective-permute-done((f32[16,128,128]{2,1,0:T(8,128)}, f32[16,128,128]{2,1,0:T(8,128)S(1)}, u32[]{:S(2)}, u32[]{:S(2)}) %collective-permute-start) | collective-permute-done | bytes 1048608 | tf_op jit(solution)/shard_map/while/body/eval_jaxpr/ppermute | solution.py:10
  1376.8 8.1 fusion.118
  1384.9 34.7 %collective-permute-done = f32[16,128,128]{2,1,0:T(8,128)S(1)} collective-permute-done((f32[16,128,128]{2,1,0:T(8,128)}, f32[16,128,128]{2,1,0:T(8,128)S(1)}, u32[]{:S(2)}, u32[]{:S(2)}) %collective-permute-start) | collective-permute-done | bytes 1048608 | tf_op jit(solution)/shard_map/while/body/eval_jaxpr/ppermute | solution.py:10
  1428.3 8.1 fusion.118
  1436.4 16.5 collective-permute-done
  1461.6 8.1 fusion.118
  1469.7 16.5 collective-permute-done
  1494.9 8.1 fusion.118
  1503.0 16.6 collective-permute-done
  1528.3 8.1 fusion.118
  1536.4 16.5 collective-permute-done
  1561.6 8.1 fusion.118
  1569.7 16.5 collective-permute-done
  1594.9 8.1 fusion.118
  1603.0 16.5 collective-permute-done
  1628.3 8.1 fusion.118
  1636.4 16.5 collective-permute-done
  1661.6 8.1 fusion.118
  1669.7 16.5 collective-permute-done
  1703.0 16.5 collective-permute-done
  1728.3 8.1 fusion.118
  1736.4 16.5 collective-permute-done
  1769.7 16.5 collective-permute-done
  1794.5 225.9 %reduce-scatter.2.cloned.1.call-done = f32[128,128]{1,0:T(8,128)} async-done(((f32[2048,128]{1,0:T(8,128)}), f32[128,128]{1,0:T(8,128)}) %reduce-scatter.2.cloned.1.call-update) | async-done | bytes 65552 | tf_op jit(solution)/shard_map/reduce_scatter | solution.py:108
  (455 shorter events, 176.3 us)
Async XLA Ops:
  6.5 1166.3 %copy-start.1 = (bf16[1024,128]{1,0:T(8,128)(2,1)S(1)}, bf16[1024,128]{1,0:T(8,128)(2,1)}, u32[]{:S(2)}) copy-start(bf16[1024,128]{1,0:T(8,128)(2,1)} %param.20) | copy-start | bytes 786436
  6.5 2013.9 %reduce-scatter.2.cloned.1.call-start = ((), (), s32[]{:S(2)}) async-start(), calls=%async_computation.1 | async-start | bytes 1114112 | tf_op jit(solution)/shard_map/reduce_scatter | solution.py:108
  1172.8 2.2 copy-start.3
  1172.8 6.7 copy-start.4
  1175.0 5.9 copy-start.2
  1175.0 6.5 copy-start
  1175.6 9.1 copy-start.6
  1200.5 40.0 %collective-permute-start = (f32[16,128,128]{2,1,0:T(8,128)}, f32[16,128,128]{2,1,0:T(8,128)S(1)}, u32[]{:S(2)}, u32[]{:S(2)}) collective-permute-start(f32[16,128,128]{2,1,0:T(8,128)} %fusion.118), channel_id=1, source_target_pairs={{240,0},{0,16},{16,32},{32,48},{48,64},{64,80},{80,96},{96,112},{1... | collective-permute-start | bytes 3145736 | tf_op jit(solution)/shard_map/while/body/eval_jaxpr/ppermute | solution.py:10
  1240.5 1.0 copy-start.5
  1257.3 34.7 %collective-permute-start = (f32[16,128,128]{2,1,0:T(8,128)}, f32[16,128,128]{2,1,0:T(8,128)S(1)}, u32[]{:S(2)}, u32[]{:S(2)}) collective-permute-start(f32[16,128,128]{2,1,0:T(8,128)} %fusion.118), channel_id=1, source_target_pairs={{240,0},{0,16},{16,32},{32,48},{48,64},{64,80},{80,96},{96,112},{1... | collective-permute-start | bytes 3145736 | tf_op jit(solution)/shard_map/while/body/eval_jaxpr/ppermute | solution.py:10
  1308.8 59.3 %collective-permute-start = (f32[16,128,128]{2,1,0:T(8,128)}, f32[16,128,128]{2,1,0:T(8,128)S(1)}, u32[]{:S(2)}, u32[]{:S(2)}) collective-permute-start(f32[16,128,128]{2,1,0:T(8,128)} %fusion.118), channel_id=1, source_target_pairs={{240,0},{0,16},{16,32},{32,48},{48,64},{64,80},{80,96},{96,112},{1... | collective-permute-start | bytes 3145736 | tf_op jit(solution)/shard_map/while/body/eval_jaxpr/ppermute | solution.py:10
  1368.1 1.0 copy-start.5
  1384.9 34.7 %collective-permute-start = (f32[16,128,128]{2,1,0:T(8,128)}, f32[16,128,128]{2,1,0:T(8,128)S(1)}, u32[]{:S(2)}, u32[]{:S(2)}) collective-permute-start(f32[16,128,128]{2,1,0:T(8,128)} %fusion.118), channel_id=1, source_target_pairs={{240,0},{0,16},{16,32},{32,48},{48,64},{64,80},{80,96},{96,112},{1... | collective-permute-start | bytes 3145736 | tf_op jit(solution)/shard_map/while/body/eval_jaxpr/ppermute | solution.py:10
  1419.6 1.0 copy-start.5
  1436.4 16.5 collective-permute-start
  1452.9 1.0 copy-start.5
  1469.7 16.5 collective-permute-start
  1486.2 1.0 copy-start.5
  1503.0 16.6 collective-permute-start
  1536.4 16.5 collective-permute-start
  1569.7 16.6 collective-permute-start
  1603.0 16.5 collective-permute-start
  1619.6 1.0 copy-start.5
  1636.4 16.5 collective-permute-start
  1669.7 16.5 collective-permute-start
  1686.2 1.0 copy-start.5
  1703.0 16.6 collective-permute-start
  1719.6 1.0 copy-start.5
  1736.4 16.5 collective-permute-start
  1769.7 16.5 collective-permute-start
  1786.2 1.0 copy-start.5
  1787.2 233.2 %copy-start.7 = (f32[128,128]{1,0:T(8,128)S(1)}, f32[128,128]{1,0:T(8,128)}, u32[]{:S(2)}) copy-start(f32[128,128]{1,0:T(8,128)} %param.21) | copy-start | bytes 196612
  (6 other events, 6.0 us)
Sparse Core Ops, SparseCore 0:
  1794.7 225.7 reduce-scatter.1
where the time goes:
time: 2030 us
  blocking collectives  1160 us (57%)
  waiting for transfers between devices  576 us (28%)
  local copies, waits for them, and re-layouts  138 us (7%)
  matrix products  129 us (6%)
    all_gather x1, blocking collectives, shards(): lax.all_gather(recv_pos, ('blk', 'lane'), axis=1, tiled=True)  594 us
    all_gather x1, blocking collectives, shards(): lax.all_gather(recv_angles, ('blk', 'lane'), axis=1, tiled=True)  562 us
    ppermute x15, waiting for transfers between devices, shifted(): return lax.ppermute(block, axis, route)  350 us
    reduce_scatter x1, waiting for transfers between devices, shards(): lax.psum_scatter(running.reshape(lane_count * block_rows, bin_count), 'la...  226 us
    dot_general x16, matrix products, contribution(): jnp.einsum('jrcs,jcsb->jrb', values, picked_flux, preferred_element_type=...  129 us
  transfers between devices with their start and end apart: 16, of which 16 were waited for; matrix products, arithmetic and copies ran while one was open for 0% of the time, Pallas kernels for 0%

commit v1 on v0

--- a/solution.py
+++ b/solution.py
@@ -2,6 +2,18 @@
 import jax.numpy as jnp
 from jax import lax
 from jax.sharding import PartitionSpec as P
+
+
+def touch_bars(local, in_dim):
+    return jnp.concatenate(
+        jax.lax.all_to_all(
+            jnp.stack([local for _ in range(jax.lax.axis_size(("blk", "lane")))]),
+            ("blk", "lane"),
+            0,
+            0,
+        ),
+        axis=in_dim,
+    )
 
 
 def shifted(block, axis, distance):
@@ -52,7 +64,7 @@
     source_blocks = src_area.shape[0] // block_rows
     slot_count = visible_lists.shape[-1]
     every_pos, every_angles = (
-        lax.all_gather(recv_pos, ("blk", "lane"), axis=1, tiled=True),
+        touch_bars(recv_pos, 1),
         lax.all_gather(recv_angles, ("blk", "lane"), axis=1, tiled=True),
     )
     receiver_pos = every_pos.reshape(3, group_count * lane_count, block_rows)

time: 2030 us -> 1380 us (0.68)
  blocking collectives: 1160 us -> 562 us
  waiting for transfers between devices: 576 us -> 505 us
    all_gather x1 -> x0, blocking collectives: 594 us -> none  [shards(): lax.all_gather(recv_pos, ('blk', 'lane'), axis=1, tiled=True)]
    ppermute x15, waiting for transfers between devices: 350 us -> 281 us  [shifted(): return lax.ppermute(block, axis, route)]
  transfers between devices with their start and end apart: 16 -> 17, of which waited for: 16 -> 16; matrix products, arithmetic and copies ran while one was open for 0% -> 1% of each run, Pallas kernels for 0% -> 0%
where the time goes in v1:
time: 1380 us
  blocking collectives  562 us (41%)
  waiting for transfers between devices  505 us (37%)
  local copies, waits for them, and re-layouts  139 us (10%)
  matrix products  129 us (9%)
  starting transfers between devices  15.8 us (1%)
    all_gather x1, blocking collectives, shards(): lax.all_gather(recv_angles, ('blk', 'lane'), axis=1, tiled=True)  562 us
    ppermute x15, waiting for transfers between devices, shifted(): return lax.ppermute(block, axis, route)  281 us
    reduce_scatter x1, waiting for transfers between devices, shards(): lax.psum_scatter(running.reshape(lane_count * block_rows, bin_count), 'la...  224 us
    dot_general x16, matrix products, contribution(): jnp.einsum('jrcs,jcsb->jrb', values, picked_flux, preferred_element_type=...  129 us
  transfers between devices with their start and end apart: 17, of which 16 were waited for; matrix products, arithmetic and copies ran while one was open for 1% of the time, Pallas kernels for 0%

profile of v1, /device:TPU:2, one launch (start us, length us, event | category | flops | bytes accessed | tf_op | source)
XLA Modules:
  0.0 1379.7 jit_solution(9884438744896925294)
XLA Ops:
  8.1 15.7 %all-to-all-start = ((f32[256,3,128]{2,1,0:T(4,128)}), f32[256,3,128]{2,1,0:T(4,128)}, u32[]{:S(2)}, u32[]{:S(2)}) async-start(f32[256,3,128]{2,1,0:T(4,128)} %stack.22), calls=%async_computation | async-start | bytes 1048576 | tf_op jit(solution)/shard_map/all_to_all | solution.py:9
  24.8 561.8 %all_gather.3 = f32[2,32768]{1,0:T(2,128)S(1)} all-gather(f32[2,128]{1,0:T(2,128)} %param.15), channel_id=1, replica_groups=mesh['blk'=16,'lane'=16] {'blk','lane'}, dimensions={1}, use_global_device_ids=true | all-gather | bytes 263168 | tf_op jit(solution)/shard_map/all_gather | solution.py:68
  607.2 533.0 %while.17 = (s32[]{:T(128)}, f32[16,128,128]{2,1,0:T(8,128)}, s32[]{:T(128)}, s32[16,16]{1,0:T(8,128)S(1)}, s32[16,16,4]{2,1,0:T(8,128)S(1)}, /*index=5*/f32[8,1...) while((s32[]{:T(128)}, f32[16,128,128]{2,1,0:T(8,128)}, ...), condition=%wide.region_1.3_spmd.clone.clone, body=%wide.region_0.2_spmd.clone.clone.sunk | while | flops 299129344 | bytes 18412892 | solution.py:118
  614.9 8.1 fusion.118
  623.0 15.3 %collective-permute-done = f32[16,128,128]{2,1,0:T(8,128)S(1)} collective-permute-done((f32[16,128,128]{2,1,0:T(8,128)}, f32[16,128,128]{2,1,0:T(8,128)S(1)}, u32[]{:S(2)}, u32[]{:S(2)}) %collective-permute-start) | collective-permute-done | bytes 1048608 | tf_op jit(solution)/shard_map/while/body/eval_jaxpr/ppermute | solution.py:22
  647.0 8.1 fusion.118
  655.1 15.3 %collective-permute-done = f32[16,128,128]{2,1,0:T(8,128)S(1)} collective-permute-done((f32[16,128,128]{2,1,0:T(8,128)}, f32[16,128,128]{2,1,0:T(8,128)S(1)}, u32[]{:S(2)}, u32[]{:S(2)}) %collective-permute-start) | collective-permute-done | bytes 1048608 | tf_op jit(solution)/shard_map/while/body/eval_jaxpr/ppermute | solution.py:22
  679.1 8.1 fusion.118
  687.2 34.1 %collective-permute-done = f32[16,128,128]{2,1,0:T(8,128)S(1)} collective-permute-done((f32[16,128,128]{2,1,0:T(8,128)}, f32[16,128,128]{2,1,0:T(8,128)S(1)}, u32[]{:S(2)}, u32[]{:S(2)}) %collective-permute-start) | collective-permute-done | bytes 1048608 | tf_op jit(solution)/shard_map/while/body/eval_jaxpr/ppermute | solution.py:22
  730.0 8.1 fusion.118
  738.1 34.7 %collective-permute-done = f32[16,128,128]{2,1,0:T(8,128)S(1)} collective-permute-done((f32[16,128,128]{2,1,0:T(8,128)}, f32[16,128,128]{2,1,0:T(8,128)S(1)}, u32[]{:S(2)}, u32[]{:S(2)}) %collective-permute-start) | collective-permute-done | bytes 1048608 | tf_op jit(solution)/shard_map/while/body/eval_jaxpr/ppermute | solution.py:22
  781.5 8.1 fusion.118
  789.6 16.5 %collective-permute-done = f32[16,128,128]{2,1,0:T(8,128)S(1)} collective-permute-done((f32[16,128,128]{2,1,0:T(8,128)}, f32[16,128,128]{2,1,0:T(8,128)S(1)}, u32[]{:S(2)}, u32[]{:S(2)}) %collective-permute-start) | collective-permute-done | bytes 1048608 | tf_op jit(solution)/shard_map/while/body/eval_jaxpr/ppermute | solution.py:22
  814.8 8.1 fusion.118
  822.9 16.5 %collective-permute-done = f32[16,128,128]{2,1,0:T(8,128)S(1)} collective-permute-done((f32[16,128,128]{2,1,0:T(8,128)}, f32[16,128,128]{2,1,0:T(8,128)S(1)}, u32[]{:S(2)}, u32[]{:S(2)}) %collective-permute-start) | collective-permute-done | bytes 1048608 | tf_op jit(solution)/shard_map/while/body/eval_jaxpr/ppermute | solution.py:22
  848.1 8.1 fusion.118
  856.2 16.6 %collective-permute-done = f32[16,128,128]{2,1,0:T(8,128)S(1)} collective-permute-done((f32[16,128,128]{2,1,0:T(8,128)}, f32[16,128,128]{2,1,0:T(8,128)S(1)}, u32[]{:S(2)}, u32[]{:S(2)}) %collective-permute-start) | collective-permute-done | bytes 1048608 | tf_op jit(solution)/shard_map/while/body/eval_jaxpr/ppermute | solution.py:22
  881.4 8.1 fusion.118
  889.5 16.5 %collective-permute-done = f32[16,128,128]{2,1,0:T(8,128)S(1)} collective-permute-done((f32[16,128,128]{2,1,0:T(8,128)}, f32[16,128,128]{2,1,0:T(8,128)S(1)}, u32[]{:S(2)}, u32[]{:S(2)}) %collective-permute-start) | collective-permute-done | bytes 1048608 | tf_op jit(solution)/shard_map/while/body/eval_jaxpr/ppermute | solution.py:22
  914.7 8.1 fusion.118
  922.8 16.5 %collective-permute-done = f32[16,128,128]{2,1,0:T(8,128)S(1)} collective-permute-done((f32[16,128,128]{2,1,0:T(8,128)}, f32[16,128,128]{2,1,0:T(8,128)S(1)}, u32[]{:S(2)}, u32[]{:S(2)}) %collective-permute-start) | collective-permute-done | bytes 1048608 | tf_op jit(solution)/shard_map/while/body/eval_jaxpr/ppermute | solution.py:22
  948.0 8.1 fusion.118
  956.1 16.5 %collective-permute-done = f32[16,128,128]{2,1,0:T(8,128)S(1)} collective-permute-done((f32[16,128,128]{2,1,0:T(8,128)}, f32[16,128,128]{2,1,0:T(8,128)S(1)}, u32[]{:S(2)}, u32[]{:S(2)}) %collective-permute-start) | collective-permute-done | bytes 1048608 | tf_op jit(solution)/shard_map/while/body/eval_jaxpr/ppermute | solution.py:22
  981.4 8.1 fusion.118
  989.5 16.5 %collective-permute-done = f32[16,128,128]{2,1,0:T(8,128)S(1)} collective-permute-done((f32[16,128,128]{2,1,0:T(8,128)}, f32[16,128,128]{2,1,0:T(8,128)S(1)}, u32[]{:S(2)}, u32[]{:S(2)}) %collective-permute-start) | collective-permute-done | bytes 1048608 | tf_op jit(solution)/shard_map/while/body/eval_jaxpr/ppermute | solution.py:22
  1014.7 8.1 fusion.118
  1022.8 16.5 %collective-permute-done = f32[16,128,128]{2,1,0:T(8,128)S(1)} collective-permute-done((f32[16,128,128]{2,1,0:T(8,128)}, f32[16,128,128]{2,1,0:T(8,128)S(1)}, u32[]{:S(2)}, u32[]{:S(2)}) %collective-permute-start) | collective-permute-done | bytes 1048608 | tf_op jit(solution)/shard_map/while/body/eval_jaxpr/ppermute | solution.py:22
  1048.0 8.1 fusion.118
  1056.1 16.5 %collective-permute-done = f32[16,128,128]{2,1,0:T(8,128)S(1)} collective-permute-done((f32[16,128,128]{2,1,0:T(8,128)}, f32[16,128,128]{2,1,0:T(8,128)S(1)}, u32[]{:S(2)}, u32[]{:S(2)}) %collective-permute-start) | collective-permute-done | bytes 1048608 | tf_op jit(solution)/shard_map/while/body/eval_jaxpr/ppermute | solution.py:22
  1089.4 16.5 %collective-permute-done = f32[16,128,128]{2,1,0:T(8,128)S(1)} collective-permute-done((f32[16,128,128]{2,1,0:T(8,128)}, f32[16,128,128]{2,1,0:T(8,128)S(1)}, u32[]{:S(2)}, u32[]{:S(2)}) %collective-permute-start) | collective-permute-done | bytes 1048608 | tf_op jit(solution)/shard_map/while/body/eval_jaxpr/ppermute | solution.py:22
  1122.7 16.5 %collective-permute-done = f32[16,128,128]{2,1,0:T(8,128)S(1)} collective-permute-done((f32[16,128,128]{2,1,0:T(8,128)}, f32[16,128,128]{2,1,0:T(8,128)S(1)}, u32[]{:S(2)}, u32[]{:S(2)}) %collective-permute-start) | collective-permute-done | bytes 1048608 | tf_op jit(solution)/shard_map/while/body/eval_jaxpr/ppermute | solution.py:22
  1147.5 223.9 %reduce-scatter.2.cloned.1.call-done = f32[128,128]{1,0:T(8,128)} async-done(((f32[2048,128]{1,0:T(8,128)}), f32[128,128]{1,0:T(8,128)}) %reduce-scatter.2.cloned.1.call-update) | async-done | bytes 65552 | tf_op jit(solution)/shard_map/reduce_scatter | solution.py:120
  (459 shorter events, 176.5 us)
Async XLA Ops:
  6.5 587.6 %copy-start.8 = (f32[2,1024]{1,0:T(2,128)S(1)}, f32[2,1024]{1,0:T(2,128)}, u32[]{:S(2)}) copy-start(f32[2,1024]{1,0:T(2,128)} %param.17) | copy-start | bytes 24580
  6.5 588.8 %copy-start.1 = (bf16[1024,128]{1,0:T(8,128)(2,1)S(1)}, bf16[1024,128]{1,0:T(8,128)(2,1)}, u32[]{:S(2)}) copy-start(bf16[1024,128]{1,0:T(8,128)(2,1)} %param.20) | copy-start | bytes 786436
  8.1 595.7 %all-to-all-start = ((f32[256,3,128]{2,1,0:T(4,128)}), f32[256,3,128]{2,1,0:T(4,128)}, u32[]{:S(2)}, u32[]{:S(2)}) async-start(f32[256,3,128]{2,1,0:T(4,128)} %stack.22), calls=%async_computation | async-start | bytes 1048576 | tf_op jit(solution)/shard_map/all_to_all | solution.py:9
  23.8 1347.6 %reduce-scatter.2.cloned.1.call-start = ((), (), s32[]{:S(2)}) async-start(), calls=%async_computation.2 | async-start | bytes 1114112 | tf_op jit(solution)/shard_map/reduce_scatter | solution.py:120
  595.3 2.2 copy-start.3
  595.3 3.5 copy-start.4
  595.3 4.2 copy-start.2
  595.3 4.8 copy-start
  598.1 9.1 copy-start.6
  623.0 15.3 %collective-permute-start = (f32[16,128,128]{2,1,0:T(8,128)}, f32[16,128,128]{2,1,0:T(8,128)S(1)}, u32[]{:S(2)}, u32[]{:S(2)}) collective-permute-start(f32[16,128,128]{2,1,0:T(8,128)} %fusion.118), channel_id=1, source_target_pairs={{240,0},{0,16},{16,32},{32,48},{48,64},{64,80},{80,96},{96,112},{1... | collective-permute-start | bytes 3145736 | tf_op jit(solution)/shard_map/while/body/eval_jaxpr/ppermute | solution.py:22
  638.4 1.0 copy-start.5
  655.1 15.3 %collective-permute-start = (f32[16,128,128]{2,1,0:T(8,128)}, f32[16,128,128]{2,1,0:T(8,128)S(1)}, u32[]{:S(2)}, u32[]{:S(2)}) collective-permute-start(f32[16,128,128]{2,1,0:T(8,128)} %fusion.118), channel_id=1, source_target_pairs={{240,0},{0,16},{16,32},{32,48},{48,64},{64,80},{80,96},{96,112},{1... | collective-permute-start | bytes 3145736 | tf_op jit(solution)/shard_map/while/body/eval_jaxpr/ppermute | solution.py:22
  670.5 1.0 copy-start.5
  687.2 34.1 %collective-permute-start = (f32[16,128,128]{2,1,0:T(8,128)}, f32[16,128,128]{2,1,0:T(8,128)S(1)}, u32[]{:S(2)}, u32[]{:S(2)}) collective-permute-start(f32[16,128,128]{2,1,0:T(8,128)} %fusion.118), channel_id=1, source_target_pairs={{240,0},{0,16},{16,32},{32,48},{48,64},{64,80},{80,96},{96,112},{1... | collective-permute-start | bytes 3145736 | tf_op jit(solution)/shard_map/while/body/eval_jaxpr/ppermute | solution.py:22
  721.4 1.0 copy-start.5
  738.1 34.7 %collective-permute-start = (f32[16,128,128]{2,1,0:T(8,128)}, f32[16,128,128]{2,1,0:T(8,128)S(1)}, u32[]{:S(2)}, u32[]{:S(2)}) collective-permute-start(f32[16,128,128]{2,1,0:T(8,128)} %fusion.118), channel_id=1, source_target_pairs={{240,0},{0,16},{16,32},{32,48},{48,64},{64,80},{80,96},{96,112},{1... | collective-permute-start | bytes 3145736 | tf_op jit(solution)/shard_map/while/body/eval_jaxpr/ppermute | solution.py:22
  772.8 1.0 copy-start.5
  789.6 16.5 %collective-permute-start = (f32[16,128,128]{2,1,0:T(8,128)}, f32[16,128,128]{2,1,0:T(8,128)S(1)}, u32[]{:S(2)}, u32[]{:S(2)}) collective-permute-start(f32[16,128,128]{2,1,0:T(8,128)} %fusion.118), channel_id=1, source_target_pairs={{240,0},{0,16},{16,32},{32,48},{48,64},{64,80},{80,96},{96,112},{1... | collective-permute-start | bytes 3145736 | tf_op jit(solution)/shard_map/while/body/eval_jaxpr/ppermute | solution.py:22
  822.9 16.5 %collective-permute-start = (f32[16,128,128]{2,1,0:T(8,128)}, f32[16,128,128]{2,1,0:T(8,128)S(1)}, u32[]{:S(2)}, u32[]{:S(2)}) collective-permute-start(f32[16,128,128]{2,1,0:T(8,128)} %fusion.118), channel_id=1, source_target_pairs={{240,0},{0,16},{16,32},{32,48},{48,64},{64,80},{80,96},{96,112},{1... | collective-permute-start | bytes 3145736 | tf_op jit(solution)/shard_map/while/body/eval_jaxpr/ppermute | solution.py:22
  839.4 1.0 copy-start.5
  856.2 16.6 %collective-permute-start = (f32[16,128,128]{2,1,0:T(8,128)}, f32[16,128,128]{2,1,0:T(8,128)S(1)}, u32[]{:S(2)}, u32[]{:S(2)}) collective-permute-start(f32[16,128,128]{2,1,0:T(8,128)} %fusion.118), channel_id=1, source_target_pairs={{240,0},{0,16},{16,32},{32,48},{48,64},{64,80},{80,96},{96,112},{1... | collective-permute-start | bytes 3145736 | tf_op jit(solution)/shard_map/while/body/eval_jaxpr/ppermute | solution.py:22
  889.5 16.5 %collective-permute-start = (f32[16,128,128]{2,1,0:T(8,128)}, f32[16,128,128]{2,1,0:T(8,128)S(1)}, u32[]{:S(2)}, u32[]{:S(2)}) collective-permute-start(f32[16,128,128]{2,1,0:T(8,128)} %fusion.118), channel_id=1, source_target_pairs={{240,0},{0,16},{16,32},{32,48},{48,64},{64,80},{80,96},{96,112},{1... | collective-permute-start | bytes 3145736 | tf_op jit(solution)/shard_map/while/body/eval_jaxpr/ppermute | solution.py:22
  906.1 1.0 copy-start.5
  922.8 16.6 %collective-permute-start = (f32[16,128,128]{2,1,0:T(8,128)}, f32[16,128,128]{2,1,0:T(8,128)S(1)}, u32[]{:S(2)}, u32[]{:S(2)}) collective-permute-start(f32[16,128,128]{2,1,0:T(8,128)} %fusion.118), channel_id=1, source_target_pairs={{240,0},{0,16},{16,32},{32,48},{48,64},{64,80},{80,96},{96,112},{1... | collective-permute-start | bytes 3145736 | tf_op jit(solution)/shard_map/while/body/eval_jaxpr/ppermute | solution.py:22
  939.4 1.0 copy-start.5
  956.1 16.5 %collective-permute-start = (f32[16,128,128]{2,1,0:T(8,128)}, f32[16,128,128]{2,1,0:T(8,128)S(1)}, u32[]{:S(2)}, u32[]{:S(2)}) collective-permute-start(f32[16,128,128]{2,1,0:T(8,128)} %fusion.118), channel_id=1, source_target_pairs={{240,0},{0,16},{16,32},{32,48},{48,64},{64,80},{80,96},{96,112},{1... | collective-permute-start | bytes 3145736 | tf_op jit(solution)/shard_map/while/body/eval_jaxpr/ppermute | solution.py:22
  989.5 16.5 %collective-permute-start = (f32[16,128,128]{2,1,0:T(8,128)}, f32[16,128,128]{2,1,0:T(8,128)S(1)}, u32[]{:S(2)}, u32[]{:S(2)}) collective-permute-start(f32[16,128,128]{2,1,0:T(8,128)} %fusion.118), channel_id=1, source_target_pairs={{240,0},{0,16},{16,32},{32,48},{48,64},{64,80},{80,96},{96,112},{1... | collective-permute-start | bytes 3145736 | tf_op jit(solution)/shard_map/while/body/eval_jaxpr/ppermute | solution.py:22
  1022.8 16.5 %collective-permute-start = (f32[16,128,128]{2,1,0:T(8,128)}, f32[16,128,128]{2,1,0:T(8,128)S(1)}, u32[]{:S(2)}, u32[]{:S(2)}) collective-permute-start(f32[16,128,128]{2,1,0:T(8,128)} %fusion.118), channel_id=1, source_target_pairs={{240,0},{0,16},{16,32},{32,48},{48,64},{64,80},{80,96},{96,112},{1... | collective-permute-start | bytes 3145736 | tf_op jit(solution)/shard_map/while/body/eval_jaxpr/ppermute | solution.py:22
  1056.1 16.6 %collective-permute-start = (f32[16,128,128]{2,1,0:T(8,128)}, f32[16,128,128]{2,1,0:T(8,128)S(1)}, u32[]{:S(2)}, u32[]{:S(2)}) collective-permute-start(f32[16,128,128]{2,1,0:T(8,128)} %fusion.118), channel_id=1, source_target_pairs={{240,0},{0,16},{16,32},{32,48},{48,64},{64,80},{80,96},{96,112},{1... | collective-permute-start | bytes 3145736 | tf_op jit(solution)/shard_map/while/body/eval_jaxpr/ppermute | solution.py:22
  1089.4 16.5 %collective-permute-start = (f32[16,128,128]{2,1,0:T(8,128)}, f32[16,128,128]{2,1,0:T(8,128)S(1)}, u32[]{:S(2)}, u32[]{:S(2)}) collective-permute-start(f32[16,128,128]{2,1,0:T(8,128)} %fusion.118), channel_id=1, source_target_pairs={{240,0},{0,16},{16,32},{32,48},{48,64},{64,80},{80,96},{96,112},{1... | collective-permute-start | bytes 3145736 | tf_op jit(solution)/shard_map/while/body/eval_jaxpr/ppermute | solution.py:22
  1122.7 16.5 %collective-permute-start = (f32[16,128,128]{2,1,0:T(8,128)}, f32[16,128,128]{2,1,0:T(8,128)S(1)}, u32[]{:S(2)}, u32[]{:S(2)}) collective-permute-start(f32[16,128,128]{2,1,0:T(8,128)} %fusion.118), channel_id=1, source_target_pairs={{240,0},{0,16},{16,32},{32,48},{48,64},{64,80},{80,96},{96,112},{1... | collective-permute-start | bytes 3145736 | tf_op jit(solution)/shard_map/while/body/eval_jaxpr/ppermute | solution.py:22
  1140.2 231.2 %copy-start.7 = (f32[128,128]{1,0:T(8,128)S(1)}, f32[128,128]{1,0:T(8,128)}, u32[]{:S(2)}) copy-start(f32[128,128]{1,0:T(8,128)} %param.21) | copy-start | bytes 196612
  (8 other events, 7.7 us)
Sparse Core Ops, SparseCore 0:
  1147.6 223.7 reduce-scatter.1
